TPU v7x, 512 devices: a whole 4x4x16 slice. The times are simulated.
512 devices in a mesh: expert: 32 (over z, core), dp: 16 (over x, y).
Axes of the slice: x: 4, y: 4, z: 16, core: 2. Of those that a mesh axis runs over, the one named last changes fastest.
Arguments:
- patches: bfloat16 [16, 32, 128, 1664], P('dp', 'expert'), may hold values from -6 to 6
- grad_out: bfloat16 [16, 32, 128, 1664], P('dp', 'expert'), may hold values from -3 to 3
- weight_in: bfloat16 [32, 1664, 4096], P('expert', None, 'dp'), may hold values from -0.15625 to 0.15625
- weight_out: bfloat16 [32, 4096, 1664], P('expert', 'dp'), may hold values from -0.09375 to 0.09375
- gates: float32 [32, 16, 32], P('expert', 'dp'), may hold values from 0.1 to 1
- counts: int32 [16, 32, 32], P(None, None, 'expert'), may hold values from 0 to 2, as said below
- picks: int32 [16, 32, 32, 2], P('dp', 'expert'), may hold values from 0 to 127, as said below
Outputs:
- grad_patches: bfloat16 [16, 32, 128, 1664], P('dp', 'expert')
- grad_weight_in: bfloat16 [32, 1664, 4096], P('expert', None, 'dp')
- grad_weight_out: bfloat16 [32, 4096, 1664], P('expert', 'dp')
Inputs may be any that keep to these rules, and one draw needn't show every extreme that they name: For each group and expert the counts over the 32 owner blocks sum to exactly 32, and in every group each expert takes 2 patches from some owner block. `picks`: for each group, owner block and expert the entries are distinct; only the first counts[g, o, e] of them are taken, the rest are arbitrary patch indices of the block.
All inputs are finite; a program needn't handle non-finite values.
Results may differ from a plain program's by a relative error of at most 0.015.
Values may be sent and summed in bfloat16 or wider, within the bound.
A program may use at most 64 MiB of HBM per device.

v0:
```python
import jax
import jax.numpy as jnp
from jax import lax
from jax.sharding import PartitionSpec as P

gelu_scale = 0.7978845608028654
gelu_cubic = 0.044715


def gelu_parts(preact):
    inner_arg = gelu_scale * (preact + gelu_cubic * preact * preact * preact)
    tangent = jnp.tanh(inner_arg)
    gelu_value = 0.5 * preact * (1.0 + tangent)
    gelu_slope = 0.5 * (1.0 + tangent) + 0.5 * preact * (1.0 - tangent * tangent) * gelu_scale * (
        1.0 + 3.0 * gelu_cubic * preact * preact
    )
    return (gelu_value, gelu_slope)


def slot_tables(owner_counts, capacity):
    owners = owner_counts.shape[-1]
    slot_ends = jnp.cumsum(owner_counts, axis=-1)
    begins = slot_ends - owner_counts
    slot_ids = jnp.arange(capacity, dtype=jnp.int32)
    owner_of = jnp.sum((slot_ends[..., None, :] <= slot_ids[:, None]).astype(jnp.int32), axis=-1)
    matches = owner_of[..., None] == jnp.arange(owners, dtype=jnp.int32)
    rank_in = slot_ids - jnp.sum(jnp.where(matches, begins[..., None, :], 0), axis=-1)
    return (owner_of, rank_in)


def on_device(patches, grad_out, weight_in, weight_out, gates, counts, picks):
    tok_local = patches.shape[2]
    dim_model = patches.shape[3]
    experts = picks.shape[2]
    per_owner = picks.shape[3]
    groups = counts.shape[0]
    owners = counts.shape[1]
    capacity = gates.shape[2]
    local_in = weight_in[0]
    local_out = weight_out[0]
    chosen = picks[0, 0].reshape(experts * per_owner)
    send_in = jnp.take(patches[0, 0], chosen, axis=0).reshape(experts, per_owner, dim_model)
    send_grad = jnp.take(grad_out[0, 0], chosen, axis=0).reshape(experts, per_owner, dim_model)
    arrived_in, arrived_grad = (
        lax.all_to_all(send_in, "expert", split_axis=0, concat_axis=0, tiled=True),
        lax.all_to_all(send_grad, "expert", split_axis=0, concat_axis=0, tiled=True),
    )
    arrived_in = arrived_in.reshape(owners * per_owner, dim_model)
    arrived_grad = arrived_grad.reshape(owners * per_owner, dim_model)
    all_counts = counts[:, :, 0]
    group_index = lax.axis_index("dp")
    my_counts = lax.dynamic_index_in_dim(all_counts, group_index, 0, keepdims=False)
    my_begins = jnp.cumsum(my_counts) - my_counts
    rank_ids = jnp.arange(per_owner, dtype=jnp.int32)
    slot_of = (my_begins[:, None] + rank_ids[None, :]).reshape(owners * per_owner)
    is_valid = (rank_ids[None, :] < my_counts[:, None]).reshape(owners * per_owner)
    my_gates = gates[0, 0]
    slot_hits = (slot_of[:, None] == jnp.arange(capacity, dtype=jnp.int32)[None, :]) & is_valid[
        :, None
    ]
    padded_gates = jnp.sum(jnp.where(slot_hits, my_gates[None, :], 0.0), axis=1)
    scaled_rows = (padded_gates[:, None] * arrived_grad.astype(jnp.float32)).astype(jnp.bfloat16)
    piece_in = lax.all_gather(arrived_in, "dp", axis=0, tiled=True)
    piece_grad = lax.all_gather(scaled_rows, "dp", axis=0, tiled=True)
    preact = jnp.dot(piece_in, local_in, preferred_element_type=jnp.float32)
    gelu_value, gelu_slope = gelu_parts(preact)
    hidden = gelu_value.astype(jnp.bfloat16)
    grad_hidden = lax.dot_general(
        piece_grad, local_out, (((1,), (1,)), ((), ())), preferred_element_type=jnp.float32
    )
    grad_pre = (grad_hidden * gelu_slope).astype(jnp.bfloat16)
    sum_out = lax.dot_general(
        hidden, piece_grad, (((0,), (0,)), ((), ())), preferred_element_type=jnp.float32
    )
    sum_in = lax.dot_general(
        piece_in, grad_pre, (((0,), (0,)), ((), ())), preferred_element_type=jnp.float32
    )
    sum_in, sum_out, grad_stash = (sum_in, sum_out, grad_pre)
    owner_all, rank_all = slot_tables(all_counts, capacity)
    group_base = jnp.arange(groups, dtype=jnp.int32)[:, None] * (owners * per_owner)
    padded_index = (group_base + owner_all * per_owner + rank_all).reshape(groups * capacity)
    stash_rows = jnp.take(grad_stash, padded_index, axis=0)
    expert_grad = lax.psum_scatter(
        lax.dot_general(
            stash_rows, local_in, (((1,), (1,)), ((), ())), preferred_element_type=jnp.float32
        ).astype(jnp.bfloat16),
        "dp",
        scatter_dimension=0,
        tiled=True,
    )
    returned = jnp.take(expert_grad, jnp.clip(slot_of, 0, capacity - 1), axis=0)
    returned = jnp.where(is_valid[:, None], returned, jnp.zeros_like(returned))
    returned = returned.reshape(owners, per_owner, dim_model)
    arrived_back = lax.all_to_all(returned, "expert", split_axis=0, concat_axis=0, tiled=True)
    arrived_back = arrived_back.reshape(experts * per_owner, dim_model)
    owner_table = (jnp.arange(tok_local, dtype=jnp.int32)[:, None] == chosen[None, :]).astype(
        jnp.bfloat16
    )
    grad_local = jnp.dot(owner_table, arrived_back, preferred_element_type=jnp.float32).astype(
        jnp.bfloat16
    )
    return (
        grad_local[None, None],
        sum_in.astype(jnp.bfloat16)[None],
        sum_out.astype(jnp.bfloat16)[None],
    )


def solution(mesh):
    return jax.shard_map(
        on_device,
        mesh=mesh,
        in_specs=(
            P("dp", "expert", None, None),
            P("dp", "expert", None, None),
            P("expert", None, "dp"),
            P("expert", "dp", None),
            P("expert", "dp", None),
            P(None, None, "expert"),
            P("dp", "expert", None, None),
        ),
        out_specs=(P("dp", "expert", None, None), P("expert", None, "dp"), P("expert", "dp", None)),
        check_vma=False,
    )
```

profile of v0, /device:TPU:1, one launch (start us, length us, event | category | flops | bytes accessed | tf_op | source)
XLA Modules:
  0.0 311.9 jit_solution(8683857423019029709)
XLA Ops:
  7.2 0.8 copy.14
  8.1 0.1 eq.42
  8.2 2.0 gather_fusion.3
  10.2 2.0 gather_fusion.2
  12.2 0.1 broadcast_select_fusion.2
  12.4 36.1 %all_to_all.15 = bf16[32,2,1664]{2,1,0:T(2,128)(2,1)S(1)} all-to-all(bf16[32,2,1664]{2,1,0:T(2,128)(2,1)S(1)} %reshape.235), channel_id=1, replica_groups=mesh['expert'=32,'dp'=16] {'expert'}, dimensions={0} | all-to-all | bytes 425984 | tf_op jit(solution)/shard_map/all_to_all | solution.py:45
  48.6 0.8 reshape.236
  49.3 0.8 reshape.234
  50.1 4.9 %all-to-all-start = ((bf16[32,2,1664]{2,1,0:T(2,128)(2,1)}), bf16[32,2,1664]{2,1,0:T(2,128)(2,1)S(1)}, u32[]{:S(2)}, u32[]{:S(2)}) async-start(bf16[32,2,1664]{2,1,0:T(2,128)(2,1)} %reshape.234), calls=%async_computation | async-start | bytes 425984 | tf_op jit(solution)/shard_map/all_to_all | solution.py:46
  55.2 0.1 reduce
  55.4 0.1 lt.83
  55.6 0.1 add.147
  55.8 18.8 %all-to-all-done = bf16[32,2,1664]{2,1,0:T(2,128)(2,1)S(1)} async-done(((bf16[32,2,1664]{2,1,0:T(2,128)(2,1)}), bf16[32,2,1664]{2,1,0:T(2,128)(2,1)S(1)}, u32[]{:S(2)}, u32[]{:S(2)}) %all-to-all-start) | async-done | bytes 213024 | tf_op jit(solution)/shard_map/all_to_all | solution.py:46
  74.7 0.8 multiply_convert_fusion.2
  75.5 0.2 reduce_window_sum.18
  75.7 0.3 convert_reduce_fusion
  76.1 0.5 select_reduce_fusion
  76.8 28.1 %all-gather.5.cloned.1.call-done = bf16[1024,1664]{1,0:T(8,128)(2,1)} async-done(((bf16[64,1664]{1,0:T(8,128)(2,1)}), bf16[1024,1664]{1,0:T(8,128)(2,1)}) %all-gather.5.cloned.1.call-update) | async-done | bytes 3407888 | tf_op jit(solution)/shard_map/all_gather | solution.py:63
  104.9 3.1 fusion.10
  108.0 63.5 %all-gather.3.cloned.1.call-done = bf16[1024,1664]{1,0:T(8,128)(2,1)} async-done(((bf16[64,1664]{1,0:T(8,128)(2,1)}), bf16[1024,1664]{1,0:T(8,128)(2,1)}) %all-gather.3.cloned.1.call-update) | async-done | bytes 3407888 | tf_op jit(solution)/shard_map/all_gather | solution.py:64
  171.5 3.5 %fusion.3 = bf16[1024,256]{1,0:T(8,128)(2,1)S(1)} fusion(bf16[1024,1664]{1,0:T(8,128)(2,1)} %all-gather.3.cloned.1.call-done, f32[1024,256]{1,0:T(8,128)S(1)} %fusion.10, bf16[1,256,1664]{2,1,0:T(8,128)(2,1)S(1)} %copy-done.4), kind=kOutput, calls=%fused_computation.14 | convolution fusion | flops 877395968 | bytes 5832704 | tf_op jit(solution)/shard_map/dot_general | solution.py:68
  174.9 2.0 gather_fusion
  176.9 1.9 convolution_convert_fusion
  178.8 0.1 min.12
  179.0 87.9 %reduce-scatter.2.cloned.1.call-done = bf16[32,1664]{1,0:T(8,128)(2,1)} async-done(((bf16[512,1664]{1,0:T(8,128)(2,1)}), bf16[32,1664]{1,0:T(8,128)(2,1)}) %reduce-scatter.2.cloned.1.call-update) | async-done | bytes 106512 | tf_op jit(solution)/shard_map/reduce_scatter | solution.py:83
  267.0 1.8 gather_fusion.1
  268.9 1.1 broadcast_select_fusion.1
  270.0 14.7 %all-to-all-start.2 = ((bf16[32,2,1664]{2,1,0:T(2,128)(2,1)}), bf16[32,2,1664]{2,1,0:T(2,128)(2,1)S(1)}, u32[]{:S(2)}, u32[]{:S(2)}) async-start(bf16[32,2,1664]{2,1,0:T(2,128)(2,1)} %broadcast_select_fusion.1), calls=%async_computation.3 | async-start | bytes 425984 | tf_op jit(solution)/shard_map/all_to_all | solution.py:94
  284.7 4.1 %fusion = bf16[1,1664,256]{2,1,0:T(8,128)(2,1)} fusion(bf16[1024,1664]{1,0:T(8,128)(2,1)} %all-gather.5.cloned.1.call-done, bf16[1024,256]{1,0:T(8,128)(2,1)S(1)} %fusion.3), kind=kOutput, calls=%fused_computation.7 | convolution fusion | flops 872841216 | bytes 4784128 | tf_op jit(solution)/shard_map/dot_general | solution.py:75
  288.8 2.1 fusion.1
  290.9 13.3 %all-to-all-done.2 = bf16[32,2,1664]{2,1,0:T(2,128)(2,1)S(1)} async-done(((bf16[32,2,1664]{2,1,0:T(2,128)(2,1)}), bf16[32,2,1664]{2,1,0:T(2,128)(2,1)S(1)}, u32[]{:S(2)}, u32[]{:S(2)}) %all-to-all-start.2) | async-done | bytes 213024 | tf_op jit(solution)/shard_map/all_to_all | solution.py:94
  304.3 1.0 fusion.2
  (41 shorter events, 1.3 us)
Async XLA Ops:
  7.2 97.7 %copy-start = (bf16[1,1664,256]{2,1,0:T(8,128)(2,1)S(1)}, bf16[1,1664,256]{2,1,0:T(8,128)(2,1)}, u32[]{:S(2)}) copy-start(bf16[1,1664,256]{2,1,0:T(8,128)(2,1)} %param.11) | copy-start | bytes 2555908
  7.2 97.7 %all-gather.5.cloned.1.call-start = ((), (), s32[]{:S(2)}) async-start(), calls=%async_computation.5 | async-start | bytes 3620864 | tf_op jit(solution)/shard_map/all_gather | solution.py:63
  8.2 46.8 %copy-start.1 = (s32[16,32,1]{1,2,0:T(1,128)S(1)}, s32[16,32,1]{1,2,0:T(1,128)}, u32[]{:S(2)}) copy-start(s32[16,32,1]{1,2,0:T(1,128)} %param.14) | copy-start | bytes 6148
  8.2 47.5 %copy-start.2 = (f32[1,1,32]{2,1,0:T(1,128)S(1)}, f32[1,1,32]{2,1,0:T(1,128)}, u32[]{:S(2)}) copy-start(f32[1,1,32]{2,1,0:T(1,128)} %param.13) | copy-start | bytes 388
  50.1 24.5 %all-to-all-start = ((bf16[32,2,1664]{2,1,0:T(2,128)(2,1)}), bf16[32,2,1664]{2,1,0:T(2,128)(2,1)S(1)}, u32[]{:S(2)}, u32[]{:S(2)}) async-start(bf16[32,2,1664]{2,1,0:T(2,128)(2,1)} %reshape.234), calls=%async_computation | async-start | bytes 425984 | tf_op jit(solution)/shard_map/all_to_all | solution.py:46
  55.0 116.5 %all-gather.3.cloned.1.call-start = ((), (), s32[]{:S(2)}) async-start(), calls=%async_computation.4 | async-start | bytes 3620864 | tf_op jit(solution)/shard_map/all_gather | solution.py:64
  75.5 191.5 %reduce-scatter.2.cloned.1.call-start = ((), (), s32[]{:S(2)}) async-start(), calls=%async_computation.6 | async-start | bytes 1810432 | tf_op jit(solution)/shard_map/reduce_scatter | solution.py:83
  76.8 94.6 %copy-start.4 = (bf16[1,256,1664]{2,1,0:T(8,128)(2,1)S(1)}, bf16[1,256,1664]{2,1,0:T(8,128)(2,1)}, u32[]{:S(2)}) copy-start(bf16[1,256,1664]{2,1,0:T(8,128)(2,1)} %param.12) | copy-start | bytes 2555908
  270.0 34.3 %all-to-all-start.2 = ((bf16[32,2,1664]{2,1,0:T(2,128)(2,1)}), bf16[32,2,1664]{2,1,0:T(2,128)(2,1)S(1)}, u32[]{:S(2)}, u32[]{:S(2)}) async-start(bf16[32,2,1664]{2,1,0:T(2,128)(2,1)} %broadcast_select_fusion.1), calls=%async_computation.3 | async-start | bytes 425984 | tf_op jit(solution)/shard_map/all_to_all | solution.py:94
  284.7 4.1 %copy-start.3 = (bf16[1024,1664]{1,0:T(8,128)(2,1)S(1)}, bf16[1024,1664]{1,0:T(8,128)(2,1)}, u32[]{:S(2)}) copy-start(bf16[1024,1664]{1,0:T(8,128)(2,1)} %all-gather.3.cloned.1.call-done) | copy-start | bytes 10223620
Sparse Core Ops, SparseCore 0:
  49.5 55.3 all-gather.4
  108.5 62.8 all-gather.2
  179.0 87.9 reduce-scatter.1
where the time goes:
time: 312 us
  waiting for transfers between devices  212 us (68%)
  blocking collectives  36.1 us (12%)
  starting transfers between devices  19.7 us (6%)
  matrix products  15.7 us (5%)
  between operations  14 us (4%)
  local copies, waits for them, and re-layouts  11.2 us (4%)
  other arithmetic  3.6 us (1%)
    reduce_scatter x1, waiting for transfers between devices, on_device(): lax.psum_scatter(lax.dot_general(stash_rows, local_in, (((1,), (1,)), (()...  87.9 us
    all_gather x1, waiting for transfers between devices, on_device(): piece_grad = lax.all_gather(scaled_rows, 'dp', axis=0, tiled=True)  63.5 us
    all_to_all x1, blocking collectives, on_device(): lax.all_to_all(send_in, 'expert', split_axis=0, concat_axis=0, tiled=True)  36.1 us
    all_gather x1, waiting for transfers between devices, on_device(): piece_in = lax.all_gather(arrived_in, 'dp', axis=0, tiled=True)  28.1 us
    all_to_all x1, waiting for transfers between devices, on_device(): lax.all_to_all(send_grad, 'expert', split_axis=0, concat_axis=0, tiled=True)  18.8 us
    all_to_all x1, starting transfers between devices, on_device(): lax.all_to_all(returned, 'expert', split_axis=0, concat_axis=0, tiled=True)  14.7 us
    all_to_all x1, waiting for transfers between devices, on_device(): lax.all_to_all(returned, 'expert', split_axis=0, concat_axis=0, tiled=True)  13.3 us
  transfers between devices with their start and end apart: 5, of which 5 were waited for; matrix products, arithmetic and copies ran while one was open for 4% of the time, Pallas kernels for 0%

commit v1 on v0

--- a/solution.py
+++ b/solution.py
@@ -61,7 +61,9 @@
     padded_gates = jnp.sum(jnp.where(slot_hits, my_gates[None, :], 0.0), axis=1)
     scaled_rows = (padded_gates[:, None] * arrived_grad.astype(jnp.float32)).astype(jnp.bfloat16)
     piece_in = lax.all_gather(arrived_in, "dp", axis=0, tiled=True)
-    piece_grad = lax.all_gather(scaled_rows, "dp", axis=0, tiled=True)
+    piece_grad = jnp.concatenate(
+        lax.all_to_all(jnp.stack([scaled_rows] * lax.axis_size("dp")), "dp", 0, 0), axis=0
+    )
     preact = jnp.dot(piece_in, local_in, preferred_element_type=jnp.float32)
     gelu_value, gelu_slope = gelu_parts(preact)
     hidden = gelu_value.astype(jnp.bfloat16)

time: 312 us -> 279 us (0.89)
  waiting for transfers between devices: 212 us -> 168 us
  starting transfers between devices: 19.7 us -> 26.4 us
    all_gather x1 -> x0, waiting for transfers between devices: 63.5 us -> none  [on_device(): piece_grad = lax.all_gather(scaled_rows, 'dp', axis=0, tiled=True)]
    all_gather x1, waiting for transfers between devices: 28.1 us -> 56 us  [on_device(): piece_in = lax.all_gather(arrived_in, 'dp', axis=0, tiled=True)]
    all_to_all x0 -> x1, starting transfers between devices: none -> 6.8 us  [on_device(): lax.all_to_all(jnp.stack([scaled_rows] * lax.axis_size('dp')), 'dp', 0, 0)]
    reduce_scatter x1, waiting for transfers between devices: 87.9 us -> 81.5 us  [on_device(): lax.psum_scatter(lax.dot_general(stash_rows, local_in, (((1,), (1,)), (()...]
  transfers between devices with their start and end apart: 5 -> 5, of which waited for: 5 -> 4; matrix products, arithmetic and copies ran while one was open for 4% -> 6% of each run, Pallas kernels for 0% -> 0%
where the time goes in v1:
time: 279 us; the launch traced here: 278 us
  waiting for transfers between devices  168 us (60%)
  blocking collectives  36.1 us (13%)
  starting transfers between devices  26.4 us (9%)
  matrix products  17.5 us (6%)
  between operations  14.3 us (5%)
  local copies, waits for them, and re-layouts  13.3 us (5%)
  other arithmetic  2.92 us (1%)
    reduce_scatter x1, waiting for transfers between devices, on_device(): lax.psum_scatter(lax.dot_general(stash_rows, local_in, (((1,), (1,)), (()...  81.5 us
    all_gather x1, waiting for transfers between devices, on_device(): piece_in = lax.all_gather(arrived_in, 'dp', axis=0, tiled=True)  56 us
    all_to_all x1, blocking collectives, on_device(): lax.all_to_all(send_in, 'expert', split_axis=0, concat_axis=0, tiled=True)  36.1 us
    all_to_all x1, waiting for transfers between devices, on_device(): lax.all_to_all(send_grad, 'expert', split_axis=0, concat_axis=0, tiled=True)  18.9 us
    all_to_all x1, starting transfers between devices, on_device(): lax.all_to_all(returned, 'expert', split_axis=0, concat_axis=0, tiled=True)  14.6 us
    all_to_all x1, waiting for transfers between devices, on_device(): lax.all_to_all(returned, 'expert', split_axis=0, concat_axis=0, tiled=True)  11.5 us
    all_to_all x1, starting transfers between devices, on_device(): lax.all_to_all(jnp.stack([scaled_rows] * lax.axis_size('dp')), 'dp', 0, 0)  6.8 us
  transfers between devices with their start and end apart: 5, of which 4 were waited for; matrix products, arithmetic and copies ran while one was open for 6% of the time, Pallas kernels for 0%

profile of v1, /device:TPU:1, one launch (start us, length us, event | category | flops | bytes accessed | tf_op | source)
XLA Modules:
  0.0 278.5 jit_solution(2804326243128290287)
XLA Ops:
  7.2 0.8 copy.14
  8.1 0.1 eq.42
  8.2 2.0 gather_fusion.2
  10.2 2.0 gather_fusion.3
  12.2 0.1 broadcast_select_fusion.2
  12.4 36.1 %all_to_all.20 = bf16[32,2,1664]{2,1,0:T(2,128)(2,1)S(1)} all-to-all(bf16[32,2,1664]{2,1,0:T(2,128)(2,1)S(1)} %reshape.248), channel_id=1, replica_groups=mesh['expert'=32,'dp'=16] {'expert'}, dimensions={0} | all-to-all | bytes 425984 | tf_op jit(solution)/shard_map/all_to_all | solution.py:45
  48.6 0.8 reshape.249
  49.3 0.8 reshape.246
  50.1 4.9 %all-to-all-start = ((bf16[32,2,1664]{2,1,0:T(2,128)(2,1)}), bf16[32,2,1664]{2,1,0:T(2,128)(2,1)S(1)}, u32[]{:S(2)}, u32[]{:S(2)}) async-start(bf16[32,2,1664]{2,1,0:T(2,128)(2,1)} %reshape.246), calls=%async_computation | async-start | bytes 425984 | tf_op jit(solution)/shard_map/all_to_all | solution.py:46
  55.2 0.1 reduce
  55.4 0.1 add.147
  55.5 0.1 lt.83
  55.8 18.9 %all-to-all-done = bf16[32,2,1664]{2,1,0:T(2,128)(2,1)S(1)} async-done(((bf16[32,2,1664]{2,1,0:T(2,128)(2,1)}), bf16[32,2,1664]{2,1,0:T(2,128)(2,1)S(1)}, u32[]{:S(2)}, u32[]{:S(2)}) %all-to-all-start) | async-done | bytes 213024 | tf_op jit(solution)/shard_map/all_to_all | solution.py:46
  74.8 2.1 stack.2
  76.9 6.8 %all-to-all-start.1 = ((bf16[16,64,1664]{2,1,0:T(8,128)(2,1)}), bf16[16,64,1664]{2,1,0:T(8,128)(2,1)}, u32[]{:S(2)}, u32[]{:S(2)}) async-start(bf16[16,64,1664]{2,1,0:T(8,128)(2,1)} %stack.2), calls=%async_computation.1 | async-start | bytes 6815744 | tf_op jit(solution)/shard_map/all_to_all | solution.py:65
  83.8 0.2 reduce_window_sum.18
  84.0 0.3 convert_reduce_fusion
  84.3 0.5 select_reduce_fusion
  85.1 56.0 %all-gather.2.cloned.1.call-done = bf16[1024,1664]{1,0:T(8,128)(2,1)} async-done(((bf16[64,1664]{1,0:T(8,128)(2,1)}), bf16[1024,1664]{1,0:T(8,128)(2,1)}) %all-gather.2.cloned.1.call-update) | async-done | bytes 3407888 | tf_op jit(solution)/shard_map/all_gather | solution.py:63
  141.1 3.1 %fusion.10 = f32[1024,256]{1,0:T(8,128)S(1)} fusion(bf16[1024,1664]{1,0:T(8,128)(2,1)} %all-gather.2.cloned.1.call-done, bf16[1,1664,256]{2,1,0:T(8,128)(2,1)S(1)} %copy-done), kind=kOutput, calls=%fused_computation.22 | convolution fusion | flops 872415232 | bytes 5308416 | tf_op jit(solution)/shard_map/dot_general | solution.py:67
  144.2 3.5 %fusion.3 = bf16[1024,256]{1,0:T(8,128)(2,1)S(1)} fusion(bf16[1024,1664]{1,0:T(8,128)(2,1)} %bitcast.5, f32[1024,256]{1,0:T(8,128)S(1)} %fusion.10, bf16[1,256,1664]{2,1,0:T(8,128)(2,1)S(1)} %copy-done.3), kind=kOutput, calls=%fused_computation.14 | convolution fusion | flops 877395968 | bytes 5832704 | tf_op jit(solution)/shard_map/dot_general | solution.py:70
  147.7 2.0 gather_fusion
  149.6 1.9 convolution_convert_fusion
  151.6 0.1 min.12
  151.8 81.5 %reduce-scatter.2.cloned.1.call-done = bf16[32,1664]{1,0:T(8,128)(2,1)} async-done(((bf16[512,1664]{1,0:T(8,128)(2,1)}), bf16[32,1664]{1,0:T(8,128)(2,1)}) %reduce-scatter.2.cloned.1.call-update) | async-done | bytes 106512 | tf_op jit(solution)/shard_map/reduce_scatter | solution.py:85
  233.3 1.8 gather_fusion.1
  235.2 1.1 broadcast_select_fusion.1
  236.3 14.6 %all-to-all-start.3 = ((bf16[32,2,1664]{2,1,0:T(2,128)(2,1)}), bf16[32,2,1664]{2,1,0:T(2,128)(2,1)S(1)}, u32[]{:S(2)}, u32[]{:S(2)}) async-start(bf16[32,2,1664]{2,1,0:T(2,128)(2,1)} %broadcast_select_fusion.1), calls=%async_computation.4 | async-start | bytes 425984 | tf_op jit(solution)/shard_map/all_to_all | solution.py:96
  251.0 4.0 %fusion = bf16[1,1664,256]{2,1,0:T(8,128)(2,1)} fusion(bf16[1024,1664]{1,0:T(8,128)(2,1)} %all-gather.2.cloned.1.call-done, bf16[1024,256]{1,0:T(8,128)(2,1)S(1)} %fusion.3), kind=kOutput, calls=%fused_computation.7 | convolution fusion | flops 872841216 | bytes 4784128 | tf_op jit(solution)/shard_map/dot_general | solution.py:77
  254.9 4.1 %fusion.1 = bf16[1,256,1664]{2,1,0:T(8,128)(2,1)} fusion(bf16[1024,1664]{1,0:T(8,128)(2,1)} %bitcast.5, f32[1024,256]{1,0:T(8,128)S(1)} %fusion.10), kind=kOutput, calls=%fused_computation.8 | convolution fusion | flops 875200512 | bytes 5308416 | tf_op jit(solution)/shard_map/dot_general | solution.py:74
  259.0 11.5 %all-to-all-done.3 = bf16[32,2,1664]{2,1,0:T(2,128)(2,1)S(1)} async-done(((bf16[32,2,1664]{2,1,0:T(2,128)(2,1)}), bf16[32,2,1664]{2,1,0:T(2,128)(2,1)S(1)}, u32[]{:S(2)}, u32[]{:S(2)}) %all-to-all-start.3) | async-done | bytes 213024 | tf_op jit(solution)/shard_map/all_to_all | solution.py:96
  270.6 1.0 fusion.2
  (39 shorter events, 1.3 us)
Async XLA Ops:
  7.2 133.9 %copy-start = (bf16[1,1664,256]{2,1,0:T(8,128)(2,1)S(1)}, bf16[1,1664,256]{2,1,0:T(8,128)(2,1)}, u32[]{:S(2)}) copy-start(bf16[1,1664,256]{2,1,0:T(8,128)(2,1)} %param.11) | copy-start | bytes 2555908
  7.2 133.9 %all-gather.2.cloned.1.call-start = ((), (), s32[]{:S(2)}) async-start(), calls=%async_computation.5 | async-start | bytes 3620864 | tf_op jit(solution)/shard_map/all_gather | solution.py:63
  8.2 46.8 %copy-start.1 = (s32[16,32,1]{1,2,0:T(1,128)S(1)}, s32[16,32,1]{1,2,0:T(1,128)}, u32[]{:S(2)}) copy-start(s32[16,32,1]{1,2,0:T(1,128)} %param.14) | copy-start | bytes 6148
  8.2 47.5 %copy-start.2 = (f32[1,1,32]{2,1,0:T(1,128)S(1)}, f32[1,1,32]{2,1,0:T(1,128)}, u32[]{:S(2)}) copy-start(f32[1,1,32]{2,1,0:T(1,128)} %param.13) | copy-start | bytes 388
  50.1 24.5 %all-to-all-start = ((bf16[32,2,1664]{2,1,0:T(2,128)(2,1)}), bf16[32,2,1664]{2,1,0:T(2,128)(2,1)S(1)}, u32[]{:S(2)}, u32[]{:S(2)}) async-start(bf16[32,2,1664]{2,1,0:T(2,128)(2,1)} %reshape.246), calls=%async_computation | async-start | bytes 425984 | tf_op jit(solution)/shard_map/all_to_all | solution.py:46
  76.9 67.2 %all-to-all-start.1 = ((bf16[16,64,1664]{2,1,0:T(8,128)(2,1)}), bf16[16,64,1664]{2,1,0:T(8,128)(2,1)}, u32[]{:S(2)}, u32[]{:S(2)}) async-start(bf16[16,64,1664]{2,1,0:T(8,128)(2,1)} %stack.2), calls=%async_computation.1 | async-start | bytes 6815744 | tf_op jit(solution)/shard_map/all_to_all | solution.py:65
  83.7 149.6 %reduce-scatter.2.cloned.1.call-start = ((), (), s32[]{:S(2)}) async-start(), calls=%async_computation.6 | async-start | bytes 1810432 | tf_op jit(solution)/shard_map/reduce_scatter | solution.py:85
  85.1 59.1 %copy-start.3 = (bf16[1,256,1664]{2,1,0:T(8,128)(2,1)S(1)}, bf16[1,256,1664]{2,1,0:T(8,128)(2,1)}, u32[]{:S(2)}) copy-start(bf16[1,256,1664]{2,1,0:T(8,128)(2,1)} %param.12) | copy-start | bytes 2555908
  236.3 34.2 %all-to-all-start.3 = ((bf16[32,2,1664]{2,1,0:T(2,128)(2,1)}), bf16[32,2,1664]{2,1,0:T(2,128)(2,1)S(1)}, u32[]{:S(2)}, u32[]{:S(2)}) async-start(bf16[32,2,1664]{2,1,0:T(2,128)(2,1)} %broadcast_select_fusion.1), calls=%async_computation.4 | async-start | bytes 425984 | tf_op jit(solution)/shard_map/all_to_all | solution.py:96
Sparse Core Ops, SparseCore 0:
  49.5 91.5 all-gather.1
  151.7 81.5 reduce-scatter.1
